TPU v7x, 128 devices: a whole 4x4x4 slice. The times are simulated.
128 devices in a mesh: seq: 64 (over y_lo, x, z, core), ch: 2 (over y_hi).
Axes of the slice: x: 4, y: 4 (y_hi: 2, y_lo: 2; y = y_hi * 2 + y_lo), z: 4, core: 2. Of those that a mesh axis runs over, the one named last changes fastest.
Arguments:
- out_grad: bfloat16 [8192, 4096], P('seq', 'ch'), may hold values from -6 to 6
- out_weight: bfloat16 [4096, 4096], P(('seq', 'ch')), may hold values from -0.09375 to 0.09375
- outer_gate: bfloat16 [8192, 4096], P('seq', 'ch'), may hold values from -6 to 6
- long_out: bfloat16 [8192, 4096], P('seq', 'ch'), may hold values from -6 to 6
- inner_gate: bfloat16 [8192, 4096], P('seq', 'ch'), may hold values from -6 to 6
- conv_input: bfloat16 [8192, 4096], P('seq', 'ch'), may hold values from -6 to 6
- short_out: bfloat16 [8192, 4096], P('seq', 'ch'), may hold values from -6 to 6
- medium_out: bfloat16 [8192, 4096], P('seq', 'ch'), may hold values from -6 to 6
- long_filter: bfloat16 [8192, 4096], P('seq', 'ch'), may hold values from -6 to 6
- taps_short: bfloat16 [7, 4096], P(None, 'ch'), may hold values from -2 to 2
- taps_medium: bfloat16 [128, 4096], P(None, 'ch'), may hold values from -0.5 to 0.5
Outputs:
- grad_outer: bfloat16 [8192, 4096], P('seq', 'ch')
- grad_inner: bfloat16 [8192, 4096], P('seq', 'ch')
- grad_input: bfloat16 [8192, 4096], P('seq', 'ch')
- grad_filter: float32 [8192, 4096], P('seq', 'ch')
- grad_short: float32 [7, 4096], P(None, 'ch')
- grad_medium: float32 [128, 4096], P(None, 'ch')
All inputs are finite; a program needn't handle non-finite values.
Results may differ from a plain program's by a relative error of at most 0.0065.
Values may be sent and summed in bfloat16 or wider, within the bound.
A program may use at most 128 MiB of HBM per device.

v0:
```python
import math
import jax
import jax.numpy as jnp
from jax import lax
from jax.sharding import PartitionSpec as P

SHORT = 7
MEDIUM = 128
ACCURATE = lax.Precision.HIGH


def from_behind(value, axis, steps):
    count = lax.axis_size(axis)
    leading, last = (max(0, -steps), min(count, count - steps))
    return lax.ppermute(value, axis, [(source, source + steps) for source in range(leading, last)])


def in_order(parts, dim):
    parts = jnp.moveaxis(parts, 0, dim)
    shape = parts.shape
    return parts.reshape(*shape[:dim], shape[dim] * shape[dim + 1], *shape[dim + 2 :])


def sent_to_all(x, axis):
    size = lax.axis_size(axis)
    return lax.all_to_all(jnp.broadcast_to(x[None], (size, *x.shape)), axis, 0, 0, tiled=True)


def gathered_copies(x, axis, dim):
    return in_order(sent_to_all(x, axis), dim)


def side_by_side(arrays, axis, split_dim, concat_dim, along):
    ends, at = ([], 0)
    for a in arrays[:-1]:
        at += a.shape[along]
        ends.append(at)
    both = jnp.concatenate(arrays, axis=along)
    return tuple(
        jnp.split(
            lax.all_to_all(both, axis, split_axis=split_dim, concat_axis=concat_dim, tiled=True),
            ends,
            axis=along,
        )
    )


def padded_to(lines, size):
    spare = -lines.shape[0] % size
    if not spare:
        return lines
    return jnp.concatenate([lines, jnp.zeros((spare, *lines.shape[1:]), lines.dtype)])


def cut_along(x, dim, size):
    before, after = (x.shape[:dim], x.shape[dim + 1 :])
    return jnp.moveaxis(x.reshape(*before, size, -1, *after), dim, 0)


def summed_on_arrival(x, axis, dim):
    size = lax.axis_size(axis)
    parts = lax.all_to_all(cut_along(x, dim, size), axis, 0, 0, tiled=True)
    return jnp.sum(parts.astype(jnp.float32), axis=0)


def total_of(x, axes):
    lines = x.reshape(-1)
    padded = padded_to(lines, lax.axis_size(axes))
    whole = gathered_copies(summed_on_arrival(padded, axes, 0).astype(jnp.bfloat16), axes, 0)
    return lax.slice_in_dim(whole, 0, len(lines)).reshape(x.shape).astype(jnp.float32)


def rotation(numer, denom):
    angles = 2.0 * math.pi / denom * numer.astype(jnp.float32)
    return (jnp.cos(angles), jnp.sin(angles))


def dft_table(length, orient):
    indices = lax.iota(jnp.int32, length)
    cosine, sine_part = rotation(indices[:, None] * indices[None, :] % length, length)
    return (cosine, orient * sine_part)


def apply_table(table, real_part, imag_part, pattern):

    def multiply(left, right):
        return jnp.einsum(pattern, left, right, precision=ACCURATE)

    if imag_part is None:
        return (multiply(table[0], real_part), multiply(table[1], real_part))
    return (
        multiply(table[0], real_part) - multiply(table[1], imag_part),
        multiply(table[0], imag_part) + multiply(table[1], real_part),
    )


def real_table(table, real_part, imag_part, pattern):
    return jnp.einsum(pattern, table[0], real_part, precision=ACCURATE) - jnp.einsum(
        pattern, table[1], imag_part, precision=ACCURATE
    )


def twist(real_part, imag_part, cosine, sine_part):
    return (real_part * cosine - imag_part * sine_part, real_part * sine_part + imag_part * cosine)


def outer_forward(signal, time_pos, row_pos, freq_pos, total):
    table = dft_table(signal.shape[0], -1.0)
    cosine, sine_part = rotation(time_pos, 2 * total)
    shift_real, shift_imag = rotation(row_pos * freq_pos % total, total)
    outputs = []
    for parity in range(2):
        if parity == 0:
            real_part, imag_part = apply_table(table, signal, None, "ca,am->cm")
        else:
            real_part, imag_part = apply_table(
                table, signal * cosine, -signal * sine_part, "ca,am->cm"
            )
        outputs += list(twist(real_part, imag_part, shift_real, -shift_imag))
    return outputs


def inner_forward(parts):
    table = dft_table(parts[0].shape[0], -1.0)
    outputs = []
    for place in range(0, len(parts), 2):
        outputs += list(apply_table(table, parts[place], parts[place + 1], "br,rn->bn"))
    return outputs


def inner_inverse(parts, narrow, total):
    table = dft_table(parts[0].shape[0], 1.0)
    row_pos = lax.iota(jnp.int32, parts[0].shape[0])[:, None]
    freq_pos = lax.iota(jnp.int32, parts[0].shape[1])[None, :] // narrow
    shift_real, shift_imag = rotation(row_pos * freq_pos % total, total)
    outputs = []
    for place in range(0, len(parts), 2):
        real_part, imag_part = apply_table(table, parts[place], parts[place + 1], "rb,bn->rn")
        outputs += list(twist(real_part, imag_part, shift_real, shift_imag))
    return outputs


def outer_inverse(parts, time_pos, total):
    table = dft_table(parts[0].shape[0], 1.0)
    cosine, sine_part = rotation(time_pos, 2 * total)
    outputs = []
    for place in range(0, len(parts), 4):
        high_real, high_imag = apply_table(table, parts[place + 2], parts[place + 3], "ac,cm->am")
        high_real, high_imag = twist(high_real, high_imag, cosine, sine_part)
        outputs.append(real_table(table, parts[place], parts[place + 1], "ac,cm->am") + high_real)
    return outputs


def conj_times(left_real, left_imag, right_real, right_imag):
    return (
        left_real * right_real + left_imag * right_imag,
        left_real * right_imag - left_imag * right_real,
    )


def spectral_terms(spectra):
    first, second = ([], [])
    for parity in range(2):
        grad_real, grad_imag = (spectra[4 + 2 * parity], spectra[5 + 2 * parity])
        point_real, point_imag = conj_times(
            spectra[8 + 2 * parity], spectra[9 + 2 * parity], grad_real, grad_imag
        )
        filt_real, filt_imag = conj_times(
            spectra[2 * parity], spectra[2 * parity + 1], grad_real, grad_imag
        )
        first += [point_real, point_imag]
        second += [filt_real, filt_imag]
    return first + second


def depthwise(signal, kernel):
    channels = signal.shape[1]
    result = lax.conv_general_dilated(
        signal.astype(jnp.float32)[None],
        kernel.astype(jnp.float32)[:, None, :],
        (1,),
        "VALID",
        dimension_numbers=("NWC", "WIO", "NWC"),
        feature_group_count=channels,
        precision=lax.Precision.HIGHEST,
    )
    return result[0]


def adjoint_taps(extended, taps):
    return depthwise(extended, taps)


def tap_products(grads, extended):
    return depthwise(extended, grads)[::-1]


def per_device(
    out_grad,
    out_weight,
    outer_gate,
    long_out,
    inner_gate,
    conv_input,
    short_out,
    medium_out,
    long_filter,
    taps_short,
    taps_medium,
):
    height = out_grad.shape[0]
    channels = outer_gate.shape[1]
    devices = lax.axis_size("seq")
    total = height * devices
    earlier_short, earlier_input = from_behind(
        (short_out[height - (MEDIUM - 1) :], conv_input[height - (SHORT - 1) :]), "seq", 1
    )
    features = gathered_copies(out_grad, "ch", 1)
    aligned = lax.all_to_all(out_weight, "ch", split_axis=1, concat_axis=0, tiled=True)
    hidden = jnp.dot(
        features,
        lax.all_gather(aligned, "seq", axis=0, tiled=True),
        preferred_element_type=jnp.float32,
    )
    grad_outer = (hidden * long_out.astype(jnp.float32)).astype(jnp.bfloat16)
    long_grad = (hidden * outer_gate.astype(jnp.float32)).astype(jnp.bfloat16)
    product = (inner_gate.astype(jnp.float32) * medium_out.astype(jnp.float32)).astype(jnp.bfloat16)
    narrow = channels // devices
    lane_span = height * narrow

    def to_blocks(signal):
        return (
            signal.reshape(height, devices, narrow).transpose(1, 0, 2).reshape(devices, lane_span)
        )

    def to_inner(signal):
        return (
            signal.reshape(devices, height, narrow)
            .transpose(1, 0, 2)
            .reshape(height, devices * narrow)
        )

    arrived = side_by_side(
        (to_blocks(product), to_blocks(long_grad), to_blocks(long_filter)), "seq", 0, 0, 1
    )
    row_pos = lax.iota(jnp.int32, lane_span)[None, :] // narrow
    source = lax.iota(jnp.int32, devices)[:, None]
    time_pos = source * height + row_pos
    spread = []
    for signal in arrived:
        spread += outer_forward(signal.astype(jnp.float32), time_pos, row_pos, source, total)
    spectra = inner_forward([to_inner(piece) for piece in spread])
    terms = inner_inverse(spectral_terms(spectra), narrow, total)
    results = outer_inverse([to_blocks(piece) for piece in terms], time_pos, total)
    result = lax.all_to_all(jnp.stack(results), "seq", split_axis=1, concat_axis=1, tiled=True)
    result = (
        result.reshape(2, devices, height, narrow)
        .transpose(0, 2, 1, 3)
        .reshape(2, height, channels)
    )
    scale = total ** (-0.5) / (2.0 * total)
    point_grad = result[0] * scale
    grad_filter = result[1] * scale
    medium_grad = (point_grad * inner_gate.astype(jnp.float32)).astype(jnp.bfloat16)
    grad_inner = (point_grad * medium_out.astype(jnp.float32)).astype(jnp.bfloat16)
    later_medium = from_behind(medium_grad[: MEDIUM - 1], "seq", -1)
    short_grad = adjoint_taps(jnp.concatenate([medium_grad, later_medium]), taps_medium).astype(
        jnp.bfloat16
    )
    later_short = from_behind(short_grad[: SHORT - 1], "seq", -1)
    grad_input = adjoint_taps(jnp.concatenate([short_grad, later_short]), taps_short).astype(
        jnp.bfloat16
    )
    partial_medium = tap_products(medium_grad, jnp.concatenate([earlier_short, short_out]))
    partial_short = tap_products(short_grad, jnp.concatenate([earlier_input, conv_input]))
    sum_medium, sum_short = (
        total_of(partial_medium.astype(jnp.bfloat16), "seq"),
        total_of(partial_short.astype(jnp.bfloat16), "seq"),
    )
    factor = total ** (-0.5)
    return (
        grad_outer,
        grad_inner,
        grad_input,
        grad_filter,
        sum_short * factor,
        sum_medium * factor,
    )


def solution(mesh):
    return jax.shard_map(
        per_device,
        mesh=mesh,
        in_specs=(
            P("seq", "ch"),
            P(("seq", "ch"), None),
            P("seq", "ch"),
            P("seq", "ch"),
            P("seq", "ch"),
            P("seq", "ch"),
            P("seq", "ch"),
            P("seq", "ch"),
            P("seq", "ch"),
            P(None, "ch"),
            P(None, "ch"),
        ),
        out_specs=(
            P("seq", "ch"),
            P("seq", "ch"),
            P("seq", "ch"),
            P("seq", "ch"),
            P(None, "ch"),
            P(None, "ch"),
        ),
        check_vma=False,
    )
```

profile of v0, /device:TPU:1, one launch (start us, length us, event | category | flops | bytes accessed | tf_op | source)
XLA Modules:
  0.0 697.4 jit_solution(6125251082649983839)
XLA Ops:
  8.2 10.4 %all_to_all.73 = bf16[32,2,2048]{2,0,1:T(8,128)(2,1)} all-to-all(bf16[32,2,2048]{2,0,1:T(8,128)(2,1)S(1)} %bitcast.295), channel_id=1, replica_groups=mesh['seq'=64,'ch'=2] {'ch'}, dimensions={1} | all-to-all | bytes 524288 | tf_op jit(solution)/shard_map/all_to_all | solution.py:219
  32.0 5.8 all-to-all-done
  37.8 109.5 %all-gather.2.cloned.1.call-done = bf16[4096,2048]{1,0:T(8,128)(2,1)} async-done(((bf16[64,2048]{1,0:T(8,128)(2,1)}), bf16[4096,2048]{1,0:T(8,128)(2,1)}) %all-gather.2.cloned.1.call-update) | async-done | bytes 16777232 | tf_op jit(solution)/shard_map/all_gather | solution.py:222
  147.2 9.3 %multiply_convert_fusion = (bf16[128,2048]{1,0:T(8,128)(2,1)}, bf16[128,2048]{1,0:T(8,128)(2,1)}) fusion(bf16[128,2048]{1,0:T(8,128)(2,1)} %param.13, bf16[128,2048]{1,0:T(8,128)(2,1)} %param.14, bf16[128,4096]{0,1:T(8,128)(2,1)S(1)} %bitcast.274, bf16[4096,2048]{1,0:T(8,128)(2,1)} %all-gather.2.cloned.1.call-done), kind=kOutput, calls=%fused_computation.128 | convolution fusion | flops 2149056512 | bytes 19922944 | tf_op jit(solution)/shard_map/dot_general | solution.py:220
  162.5 13.1 %maximum_bitcast_fusion = bf16[64,1,12288]{0,2,1:T(8,128)(2,1)} fusion(bf16[64,4096]{0,1:T(8,128)(2,1)S(1)} %bitcast.286, bf16[64,4096]{0,1:T(8,128)(2,1)} %bitcast.288, bf16[64,4096]{0,1:T(8,128)(2,1)S(1)} %bitcast.287), kind=kLoop, calls=%fused_computation.22 | loop fusion | flops 4718592 | bytes 3145728 | tf_op jit(solution)/shard_map/all_to_all | solution.py:41
  176.1 5.6 reduce.8
  186.9 6.5 all-to-all-start.2
  193.4 22.6 %all-to-all-done.2 = bf16[64,2,6144]{2,1,0:T(2,128)(2,1)S(1)} async-done(((bf16[64,2,6144]{2,1,0:T(2,128)(2,1)}), bf16[64,2,6144]{2,1,0:T(2,128)(2,1)S(1)}, u32[]{:S(2)}, u32[]{:S(2)}) %all-to-all-start.2) | async-done | bytes 1572896 | tf_op jit(solution)/shard_map/all_to_all | solution.py:41
  243.5 4.6 fusion.41
  278.0 8.8 %multiply_subtract_fusion.13 = (f32[64,4096]{1,0:T(8,128)}, f32[64,4096]{1,0:T(8,128)}, f32[64,4096]{1,0:T(8,128)S(1)}, f32[64,4096]{1,0:T(8,128)S(1)}, f32[64,4...) fusion(f32[64,4096]{1,0:T(8,128)S(1)} %fusion.118, ...), kind=kOutput, calls=%fused_computation.124 | convolution fusion | flops 114094080 | bytes 24657920 | tf_op jit(solution)/shard_map/ca,am->cm/dot_general | solution.py:87
  410.6 7.7 %multiply_add_fusion.10 = (f32[128,2048]{1,0:T(8,128)}, f32[128,2048]{1,0:T(8,128)}, f32[128,2048]{1,0:T(8,128)}, f32[128,2048]{1,0:T(8,128)}, f32[128,2048]{1,0...) fusion(f32[128,2048]{1,0:T(8,128)S(1)} %copy-done.17, ...), kind=kOutput, calls=%fused_computation.115 | convolution fusion | flops 211779584 | bytes 17833984 | tf_op jit(solution)/shard_map/rb,bn->rn/dot_general | solution.py:87
  433.0 6.6 fusion
  466.8 6.3 fusion.4
  487.9 7.4 %fusion.9 = f32[64,4096]{1,0:T(8,128)S(1)} fusion(f32[64,4096]{1,0:T(8,128)} %fusion, f32[64,4096]{1,0:T(8,128)} %fusion.207, f32[64,4096]{0,1:T(8,128)S(1)} %bitcast.229, s32[64]{0:T(128)S(1)} %iota_multiply_fusion, s32[4096]{0:T(1024)S(1)} %add_select_fusion.4), kind=kOutput, calls=%fused_computation.21 | convolution fusion | flops 102293504 | bytes 4210944 | tf_op jit(solution)/shard_map/ac,cm->am/dot_general | solution.py:87
  506.3 5.5 all-to-all-start.3
  516.6 24.1 %collective-permute-done.3 = bf16[127,2048]{1,0:T(8,128)(2,1)S(1)} collective-permute-done((bf16[127,2048]{1,0:T(8,128)(2,1)S(1)}, bf16[127,2048]{1,0:T(8,128)(2,1)S(1)}, u32[]{:S(2)}, u32[]{:S(2)}) %collective-permute-start.3) | collective-permute-done | bytes 520224 | tf_op jit(solution)/shard_map/ppermute | solution.py:15
  556.1 16.4 %fusion.11 = bf16[1,128,2048]{2,0,1:T(2,128)(2,1)S(1)} fusion(bf16[128,1,2048]{2,1,0:T(2,128)(2,1)S(1)} %copy.365, bf16[1,255,2048]{2,1,0:T(8,128)(2,1)} %maximum_bitcast_fusion.2), kind=kOutput, calls=%fused_computation.47 | convolution fusion | flops 67108864 | bytes 2093056 | tf_op jit(solution)/shard_map/conv_general_dilated | solution.py:178
  579.4 10.4 %all-to-all-start.6 = ((bf16[64,2,2048]{2,1,0:T(2,128)(2,1)}), bf16[64,2,2048]{2,1,0:T(2,128)(2,1)S(1)}, u32[]{:S(2)}, u32[]{:S(2)}) async-start(bf16[64,2,2048]{2,1,0:T(2,128)(2,1)} %reshape.352), calls=%async_computation.6 | async-start | bytes 1048576 | tf_op jit(solution)/shard_map/all_to_all | solution.py:62
  614.7 17.4 %convolution_convert_fusion = bf16[1,128,2048]{2,0,1:T(2,128)(2,1)S(1)} fusion(bf16[1,255,2048]{2,0,1:T(2,128)(2,1)} %copy.355, bf16[128,1,2048]{2,0,1:T(8,128)(2,1)S(1)} %bitcast.205), kind=kOutput, calls=%fused_computation.44 | convolution fusion | flops 67371008 | bytes 2093056 | tf_op jit(solution)/shard_map/conv_general_dilated | solution.py:178
  638.6 8.3 %all-to-all-start.4 = ((bf16[64,1,224]{2,1,0:T(2,128)(2,1)}), bf16[64,1,224]{2,1,0:T(2,128)(2,1)S(1)}, u32[]{:S(2)}, u32[]{:S(2)}) async-start(bf16[64,1,224]{2,1,0:T(2,128)(2,1)} %all_to_all.63), calls=%async_computation.4 | async-start | bytes 131072 | tf_op jit(solution)/shard_map/all_to_all | solution.py:62
  647.6 7.5 %all-to-all-done.4 = bf16[64,1,224]{2,1,0:T(2,128)(2,1)S(1)} async-done(((bf16[64,1,224]{2,1,0:T(2,128)(2,1)}), bf16[64,1,224]{2,1,0:T(2,128)(2,1)S(1)}, u32[]{:S(2)}, u32[]{:S(2)}) %all-to-all-start.4) | async-done | bytes 28704 | tf_op jit(solution)/shard_map/all_to_all | solution.py:62
  661.7 7.0 all-to-all-done.5
  668.6 4.7 all-to-all-start.7
  675.1 10.3 %all-to-all-done.7 = bf16[64,2,2048]{2,1,0:T(2,128)(2,1)S(1)} async-done(((bf16[64,2,2048]{2,1,0:T(2,128)(2,1)}), bf16[64,2,2048]{2,1,0:T(2,128)(2,1)S(1)}, u32[]{:S(2)}, u32[]{:S(2)}) %all-to-all-start.7) | async-done | bytes 524320 | tf_op jit(solution)/shard_map/all_to_all | solution.py:26
  (298 shorter events, 345.9 us)
Async XLA Ops:
  7.2 607.5 %copy-start = (bf16[128,2048]{1,0:T(8,128)(2,1)S(1)}, bf16[128,2048]{1,0:T(8,128)(2,1)}, u32[]{:S(2)}) copy-start(bf16[128,2048]{1,0:T(8,128)(2,1)} %param.21) | copy-start | bytes 1572868
  7.2 140.0 %all-gather.2.cloned.1.call-start = ((), (), s32[]{:S(2)}) async-start(), calls=%async_computation.8 | async-start | bytes 17039360 | tf_op jit(solution)/shard_map/all_gather | solution.py:222
  21.1 16.7 %all-to-all-start = ((bf16[2,128,2048]{1,2,0:T(8,128)(2,1)}), bf16[2,128,2048]{1,2,0:T(8,128)(2,1)S(1)}, u32[]{:S(2)}, u32[]{:S(2)}) async-start(bf16[2,128,2048]{1,2,0:T(8,128)(2,1)} %broadcast_in_dim.20), calls=%async_computation | async-start | bytes 2097152 | tf_op jit(solution)/shard_map/all_to_all | solution.py:26
  29.2 127.4 %copy-start.15 = (bf16[128,2048]{0,1:T(8,128)(2,1)}, bf16[128,2048]{0,1:T(8,128)(2,1)S(1)}, u32[]{:S(2)}) copy-start(bf16[128,2048]{0,1:T(8,128)(2,1)S(1)} %copy.304) | copy-start | bytes 1572868
  156.6 5.9 copy-start.35
  156.6 5.9 copy-start.36
  186.9 29.2 %all-to-all-start.2 = ((bf16[64,2,6144]{2,1,0:T(2,128)(2,1)}), bf16[64,2,6144]{2,1,0:T(2,128)(2,1)S(1)}, u32[]{:S(2)}, u32[]{:S(2)}) async-start(bf16[64,2,6144]{2,1,0:T(2,128)(2,1)} %reshape.350), calls=%async_computation.2 | async-start | bytes 3145728 | tf_op jit(solution)/shard_map/all_to_all | solution.py:41
  487.9 7.4 %copy-start.4 = (f32[64,128,32]{0,2,1:T(8,128)S(1)}, f32[64,128,32]{0,2,1:T(8,128)}, u32[]{:S(2)}) copy-start(f32[64,128,32]{0,2,1:T(8,128)} %copy-done.3) | copy-start | bytes 3145732
  487.9 7.4 %copy-start.32 = (f32[64,4096]{1,0:T(8,128)S(1)}, f32[64,4096]{1,0:T(8,128)}, u32[]{:S(2)}) copy-start(f32[64,4096]{1,0:T(8,128)} %fusion.216) | copy-start | bytes 3145732
  487.9 7.4 %copy-start.33 = (f32[64,4096]{1,0:T(8,128)S(1)}, f32[64,4096]{1,0:T(8,128)}, u32[]{:S(2)}) copy-start(f32[64,4096]{1,0:T(8,128)} %fusion.4) | copy-start | bytes 3145732
  506.3 36.5 %all-to-all-start.3 = ((f32[2,64,4096]{2,0,1:T(2,128)}), f32[2,64,4096]{2,0,1:T(2,128)S(1)}, u32[]{:S(2)}, u32[]{:S(2)}) async-start(f32[2,64,4096]{2,0,1:T(2,128)} %copy.351), calls=%async_computation.3 | async-start | bytes 4194304 | tf_op jit(solution)/shard_map/all_to_all | solution.py:255
  513.0 27.6 %collective-permute-start.3 = (bf16[127,2048]{1,0:T(8,128)(2,1)S(1)}, bf16[127,2048]{1,0:T(8,128)(2,1)S(1)}, u32[]{:S(2)}, u32[]{:S(2)}) collective-permute-start(bf16[127,2048]{1,0:T(8,128)(2,1)S(1)} %slice.29), channel_id=1, source_target_pairs={{0,2},{2,4},{4,6},{6,8},{8,10},{10,12},{12,14},{14,16},{16,18},{18... | collective-permute-start | bytes 1560584 | tf_op jit(solution)/shard_map/ppermute | solution.py:15
  553.2 56.2 %collective-permute-start = (bf16[127,2048]{0,1:T(8,128)(2,1)S(1)}, bf16[127,2048]{0,1:T(8,128)(2,1)}, u32[]{:S(2)}, u32[]{:S(2)}) collective-permute-start(bf16[127,2048]{0,1:T(8,128)(2,1)S(1)} %bitcast.275), channel_id=1, source_target_pairs={{2,0},{4,2},{6,4},{8,6},{10,8},{12,10},{14,12},{16,14},{18,16},{20... | collective-permute-start | bytes 1560584 | tf_op jit(solution)/shard_map/ppermute | solution.py:15
  574.3 23.3 %copy-start.51 = (bf16[128,2048]{0,1:T(8,128)(2,1)S(1)}, bf16[128,2048]{0,1:T(8,128)(2,1)}, u32[]{:S(2)}) copy-start(bf16[128,2048]{0,1:T(8,128)(2,1)} %get-tuple-element.71) | copy-start | bytes 1572868
  578.2 20.4 %copy-start.34 = (f32[1,128,64,32]{1,3,2,0:T(8,128)S(1)}, f32[1,128,64,32]{1,3,2,0:T(8,128)}, u32[]{:S(2)}) copy-start(f32[1,128,64,32]{1,3,2,0:T(8,128)} %get-tuple-element.64) | copy-start | bytes 3145732
  579.4 22.3 %all-to-all-start.6 = ((bf16[64,2,2048]{2,1,0:T(2,128)(2,1)}), bf16[64,2,2048]{2,1,0:T(2,128)(2,1)S(1)}, u32[]{:S(2)}, u32[]{:S(2)}) async-start(bf16[64,2,2048]{2,1,0:T(2,128)(2,1)} %reshape.352), calls=%async_computation.6 | async-start | bytes 1048576 | tf_op jit(solution)/shard_map/all_to_all | solution.py:62
  590.6 5.1 collective-permute-start.2
  614.7 19.9 %copy-start.52 = (bf16[1,134,2048]{2,1,0:T(8,128)(2,1)S(1)}, bf16[1,134,2048]{2,1,0:T(8,128)(2,1)}, u32[]{:S(2)}) copy-start(bf16[1,134,2048]{2,1,0:T(8,128)(2,1)} %maximum_bitcast_fusion.4) | copy-start | bytes 1646596
  632.2 14.7 %collective-permute-start.1 = (bf16[6,2048]{1,0:T(8,128)(2,1)S(1)}, bf16[6,2048]{1,0:T(8,128)(2,1)S(1)}, u32[]{:S(2)}, u32[]{:S(2)}) collective-permute-start(bf16[6,2048]{1,0:T(8,128)(2,1)S(1)} %bitcast.298), channel_id=1, source_target_pairs={{2,0},{4,2},{6,4},{8,6},{10,8},{12,10},{14,12},{16,14},{18,16},{20... | collective-permute-start | bytes 73736 | tf_op jit(solution)/shard_map/ppermute | solution.py:15
  638.6 16.5 %all-to-all-start.4 = ((bf16[64,1,224]{2,1,0:T(2,128)(2,1)}), bf16[64,1,224]{2,1,0:T(2,128)(2,1)S(1)}, u32[]{:S(2)}, u32[]{:S(2)}) async-start(bf16[64,1,224]{2,1,0:T(2,128)(2,1)} %all_to_all.63), calls=%async_computation.4 | async-start | bytes 131072 | tf_op jit(solution)/shard_map/all_to_all | solution.py:62
  647.0 13.4 %copy-start.55 = (bf16[7,2048]{1,0:T(8,128)(2,1)S(1)}, bf16[7,2048]{1,0:T(8,128)(2,1)}, u32[]{:S(2)}) copy-start(bf16[7,2048]{1,0:T(8,128)(2,1)} %param.20) | copy-start | bytes 86020
  647.0 13.4 %copy-start.56 = (pred[8,17]{0,1:T(8,128)(4,1)S(1)}, pred[8,17]{0,1:T(8,128)(4,1)}, u32[]{:S(2)}) copy-start(pred[8,17]{0,1:T(8,128)(4,1)} %constant.132) | copy-start | bytes 412
  655.9 12.8 %all-to-all-start.5 = ((bf16[64,1,224]{2,1,0:T(2,128)(2,1)}), bf16[64,1,224]{2,1,0:T(2,128)(2,1)S(1)}, u32[]{:S(2)}, u32[]{:S(2)}) async-start(bf16[64,1,224]{2,1,0:T(2,128)(2,1)} %broadcast_in_dim.26), calls=%async_computation.5 | async-start | bytes 131072 | tf_op jit(solution)/shard_map/all_to_all | solution.py:26
  668.6 16.8 %all-to-all-start.7 = ((bf16[64,2,2048]{2,1,0:T(2,128)(2,1)}), bf16[64,2,2048]{2,1,0:T(2,128)(2,1)S(1)}, u32[]{:S(2)}, u32[]{:S(2)}) async-start(bf16[64,2,2048]{2,1,0:T(2,128)(2,1)} %reshape.354), calls=%async_computation.7 | async-start | bytes 1048576 | tf_op jit(solution)/shard_map/all_to_all | solution.py:26
  (45 other events, 117.7 us)
Sparse Core Ops, SparseCore 0:
  18.8 128.3 all-gather.1
where the time goes:
time: 706 us; the launch traced here: 697 us
  matrix products  212 us (30%)
  waiting for transfers between devices  190 us (27%)
  local copies, waits for them, and re-layouts  175 us (25%)
  starting transfers between devices  54.8 us (8%)
  other arithmetic  39 us (6%)
  between operations  15.6 us (2%)
  blocking collectives  10.4 us (1%)
    dot_general x66, matrix products, multiply(): return jnp.einsum(pattern, left, right, precision=ACCURATE)  158 us
    all_gather x1, waiting for transfers between devices, per_device(): lax.all_gather(aligned, 'seq', axis=0, tiled=True)  109 us
    transpose x12, local copies, waits for them, and re-layouts, to_inner(): return signal.reshape(devices, height, narrow).transpose(1, 0, 2).reshape...  37.1 us
    conv_general_dilated x4, matrix products, depthwise(): lax.conv_general_dilated(signal.astype(jnp.float32)[None], kernel.astype(...  37.1 us
    transpose x11, local copies, waits for them, and re-layouts, to_blocks(): signal.reshape(height, devices, narrow).transpose(1, 0, 2)  34.3 us
    unnamed x132, local copies, waits for them, and re-layouts  27.5 us
    ppermute x4, waiting for transfers between devices, from_behind(): lax.ppermute(value, axis, [(source, source + steps) for source in range(l...  25.6 us
    sub x10, local copies, waits for them, and re-layouts, twist(): real_part * cosine - imag_part * sine_part  24.4 us
  transfers between devices with their start and end apart: 12, of which 9 were waited for; matrix products, arithmetic and copies ran while one was open for 8% of the time, Pallas kernels for 0%

commit v1 on v0

--- a/solution.py
+++ b/solution.py
@@ -219,7 +219,15 @@
     aligned = lax.all_to_all(out_weight, "ch", split_axis=1, concat_axis=0, tiled=True)
     hidden = jnp.dot(
         features,
-        lax.all_gather(aligned, "seq", axis=0, tiled=True),
+        jnp.concatenate(
+            lax.all_to_all(
+                jnp.stack([aligned for _ in range(lax.axis_size("seq"))], axis=0),
+                axis_name="seq",
+                split_axis=0,
+                concat_axis=0,
+            ),
+            axis=0,
+        ),
         preferred_element_type=jnp.float32,
     )
     grad_outer = (hidden * long_out.astype(jnp.float32)).astype(jnp.bfloat16)

time: 706 us -> 844 us (1.20)
  waiting for transfers between devices: 190 us -> 291 us
  starting transfers between devices: 54.8 us -> 94.2 us
  between operations: 15.6 us -> 2.22 us
    all_to_all x0 -> x2, waiting for transfers between devices: none -> 216 us  [the longest x1 212 us: per_device(): lax.all_to_all(jnp.stack([aligned for _ in range(lax.axis_size('seq'))],...]
    all_gather x1 -> x0, waiting for transfers between devices: 109 us -> none  [per_device(): lax.all_gather(aligned, 'seq', axis=0, tiled=True)]
    all_to_all x1, starting transfers between devices: 6.52 us -> 32.3 us  [side_by_side(): lax.all_to_all(both, axis, split_axis=split_dim, concat_axis=concat_dim,...]
    all_to_all x0 -> x2, starting transfers between devices: none -> 17.3 us  [the longest x1 12.3 us: per_device(): lax.all_to_all(jnp.stack([aligned for _ in range(lax.axis_size('seq'))],...]
    all_to_all x3 -> x2, waiting for transfers between devices: 23.1 us -> 17.3 us  [sent_to_all(): lax.all_to_all(jnp.broadcast_to(x[None], (size, *x.shape)), axis, 0, 0, t...]
  transfers between devices with their start and end apart: 12 -> 12, of which waited for: 9 -> 9; matrix products, arithmetic and copies ran while one was open for 8% -> 7% of each run, Pallas kernels for 0% -> 0%
where the time goes in v1:
time: 844 us; the launch traced here: 835 us
  waiting for transfers between devices  291 us (34%)
  matrix products  212 us (25%)
  local copies, waits for them, and re-layouts  181 us (21%)
  starting transfers between devices  94.2 us (11%)
  other arithmetic  39 us (5%)
  blocking collectives  15.5 us (2%)
    all_to_all x1, waiting for transfers between devices, per_device(): lax.all_to_all(jnp.stack([aligned for _ in range(lax.axis_size('seq'))],...  212 us
    dot_general x66, matrix products, multiply(): return jnp.einsum(pattern, left, right, precision=ACCURATE)  158 us
    transpose x12, local copies, waits for them, and re-layouts, to_inner(): return signal.reshape(devices, height, narrow).transpose(1, 0, 2).reshape...  37.1 us
    conv_general_dilated x4, matrix products, depthwise(): lax.conv_general_dilated(signal.astype(jnp.float32)[None], kernel.astype(...  37.1 us
    transpose x11, local copies, waits for them, and re-layouts, to_blocks(): signal.reshape(height, devices, narrow).transpose(1, 0, 2)  34.3 us
    all_to_all x1, starting transfers between devices, side_by_side(): lax.all_to_all(both, axis, split_axis=split_dim, concat_axis=concat_dim,...  32.3 us
    unnamed x132, local copies, waits for them, and re-layouts  27.5 us
    ppermute x4, waiting for transfers between devices, from_behind(): lax.ppermute(value, axis, [(source, source + steps) for source in range(l...  25.6 us
  transfers between devices with their start and end apart: 12, of which 9 were waited for; matrix products, arithmetic and copies ran while one was open for 7% of the time, Pallas kernels for 0%

profile of v1, /device:TPU:1, one launch (start us, length us, event | category | flops | bytes accessed | tf_op | source)
XLA Modules:
  0.0 835.0 jit_solution(6393189606294344681)
XLA Ops:
  2.4 5.0 all-to-all-start.1
  13.0 15.5 %all_to_all.75 = bf16[2,128,2048]{1,2,0:T(8,128)(2,1)S(1)} all-to-all(bf16[2,128,2048]{1,2,0:T(8,128)(2,1)S(1)} %broadcast_in_dim.20), channel_id=1, replica_groups=mesh['seq'=64,'ch'=2] {'ch'}, dimensions={0} | all-to-all | bytes 2097152 | tf_op jit(solution)/shard_map/all_to_all | solution.py:26
  28.5 5.9 stack.11
  34.5 12.3 %all-to-all-start.2 = ((bf16[64,64,2048]{2,1,0:T(8,128)(2,1)}), bf16[64,64,2048]{2,1,0:T(8,128)(2,1)}, u32[]{:S(2)}, u32[]{:S(2)}) async-start(bf16[64,64,2048]{2,1,0:T(8,128)(2,1)} %stack.11), calls=%async_computation.2 | async-start | bytes 33554432 | tf_op jit(solution)/shard_map/all_to_all | solution.py:223
  54.0 211.7 %all-to-all-done.2 = bf16[64,64,2048]{2,1,0:T(8,128)(2,1)} async-done(((bf16[64,64,2048]{2,1,0:T(8,128)(2,1)}), bf16[64,64,2048]{2,1,0:T(8,128)(2,1)}, u32[]{:S(2)}, u32[]{:S(2)}) %all-to-all-start.2) | async-done | bytes 16777248 | tf_op jit(solution)/shard_map/all_to_all | solution.py:223
  265.8 9.4 %multiply_convert_fusion = (bf16[128,2048]{1,0:T(8,128)(2,1)}, bf16[128,2048]{1,0:T(8,128)(2,1)}) fusion(bf16[128,2048]{1,0:T(8,128)(2,1)} %param.13, bf16[128,2048]{1,0:T(8,128)(2,1)} %param.14, bf16[128,4096]{0,1:T(8,128)(2,1)S(1)} %bitcast.275, bf16[4096,2048]{1,0:T(8,128)(2,1)} %bitcast.4), kind=kOutput, calls=%fused_computation.128 | convolution fusion | flops 2149056512 | bytes 19922944 | tf_op jit(solution)/shard_map/dot_general | solution.py:220
  281.0 13.1 %maximum_bitcast_fusion = bf16[64,1,12288]{0,2,1:T(8,128)(2,1)} fusion(bf16[64,4096]{0,1:T(8,128)(2,1)S(1)} %bitcast.287, bf16[64,4096]{0,1:T(8,128)(2,1)} %bitcast.289, bf16[64,4096]{0,1:T(8,128)(2,1)S(1)} %bitcast.288), kind=kLoop, calls=%fused_computation.22 | loop fusion | flops 4718592 | bytes 3145728 | tf_op jit(solution)/shard_map/all_to_all | solution.py:41
  294.6 5.6 reduce.8
  305.4 32.3 %all-to-all-start.3 = ((bf16[64,2,6144]{2,1,0:T(2,128)(2,1)}), bf16[64,2,6144]{2,1,0:T(2,128)(2,1)S(1)}, u32[]{:S(2)}, u32[]{:S(2)}) async-start(bf16[64,2,6144]{2,1,0:T(2,128)(2,1)} %reshape.357), calls=%async_computation.3 | async-start | bytes 3145728 | tf_op jit(solution)/shard_map/all_to_all | solution.py:41
  337.8 22.6 %all-to-all-done.3 = bf16[64,2,6144]{2,1,0:T(2,128)(2,1)S(1)} async-done(((bf16[64,2,6144]{2,1,0:T(2,128)(2,1)}), bf16[64,2,6144]{2,1,0:T(2,128)(2,1)S(1)}, u32[]{:S(2)}, u32[]{:S(2)}) %all-to-all-start.3) | async-done | bytes 1572896 | tf_op jit(solution)/shard_map/all_to_all | solution.py:41
  422.4 8.8 %multiply_subtract_fusion.13 = (f32[64,4096]{1,0:T(8,128)}, f32[64,4096]{1,0:T(8,128)}, f32[64,4096]{1,0:T(8,128)S(1)}, f32[64,4096]{1,0:T(8,128)S(1)}, f32[64,4...) fusion(f32[64,4096]{1,0:T(8,128)S(1)} %fusion.118, ...), kind=kOutput, calls=%fused_computation.124 | convolution fusion | flops 114094080 | bytes 24657920 | tf_op jit(solution)/shard_map/ca,am->cm/dot_general | solution.py:87
  555.0 7.7 multiply_add_fusion.10
  577.4 6.6 fusion
  611.4 6.3 fusion.4
  632.4 7.4 fusion.9
  650.8 5.5 all-to-all-start.4
  661.0 24.1 %collective-permute-done.3 = bf16[127,2048]{1,0:T(8,128)(2,1)S(1)} collective-permute-done((bf16[127,2048]{1,0:T(8,128)(2,1)S(1)}, bf16[127,2048]{1,0:T(8,128)(2,1)S(1)}, u32[]{:S(2)}, u32[]{:S(2)}) %collective-permute-start.3) | collective-permute-done | bytes 520224 | tf_op jit(solution)/shard_map/ppermute | solution.py:15
  700.5 16.4 %fusion.11 = bf16[1,128,2048]{2,0,1:T(2,128)(2,1)S(1)} fusion(bf16[128,1,2048]{2,1,0:T(2,128)(2,1)S(1)} %copy.365, bf16[1,255,2048]{2,1,0:T(8,128)(2,1)} %maximum_bitcast_fusion.2), kind=kOutput, calls=%fused_computation.47 | convolution fusion | flops 67108864 | bytes 2093056 | tf_op jit(solution)/shard_map/conv_general_dilated | solution.py:178
  723.8 10.4 %all-to-all-start.7 = ((bf16[64,2,2048]{2,1,0:T(2,128)(2,1)}), bf16[64,2,2048]{2,1,0:T(2,128)(2,1)S(1)}, u32[]{:S(2)}, u32[]{:S(2)}) async-start(bf16[64,2,2048]{2,1,0:T(2,128)(2,1)} %reshape.359), calls=%async_computation.7 | async-start | bytes 1048576 | tf_op jit(solution)/shard_map/all_to_all | solution.py:62
  759.1 17.4 %convolution_convert_fusion = bf16[1,128,2048]{2,0,1:T(2,128)(2,1)S(1)} fusion(bf16[1,255,2048]{2,0,1:T(2,128)(2,1)} %copy.355, bf16[128,1,2048]{2,0,1:T(8,128)(2,1)S(1)} %bitcast.206), kind=kOutput, calls=%fused_computation.44 | convolution fusion | flops 67371008 | bytes 2093056 | tf_op jit(solution)/shard_map/conv_general_dilated | solution.py:178
  783.0 8.3 all-to-all-start.5
  792.1 7.5 all-to-all-done.5
  806.1 7.0 all-to-all-done.6
  819.5 10.3 %all-to-all-done.8 = bf16[64,2,2048]{2,1,0:T(2,128)(2,1)S(1)} async-done(((bf16[64,2,2048]{2,1,0:T(2,128)(2,1)}), bf16[64,2,2048]{2,1,0:T(2,128)(2,1)S(1)}, u32[]{:S(2)}, u32[]{:S(2)}) %all-to-all-start.8) | async-done | bytes 524320 | tf_op jit(solution)/shard_map/all_to_all | solution.py:26
  (298 shorter events, 355.7 us)
Async XLA Ops:
  0.6 758.5 %copy-start = (bf16[128,2048]{1,0:T(8,128)(2,1)S(1)}, bf16[128,2048]{1,0:T(8,128)(2,1)}, u32[]{:S(2)}) copy-start(bf16[128,2048]{1,0:T(8,128)(2,1)} %param.21) | copy-start | bytes 1572868
  2.4 10.5 %all-to-all-start.1 = ((bf16[32,2,2048]{2,0,1:T(8,128)(2,1)}), bf16[32,2,2048]{2,0,1:T(8,128)(2,1)S(1)}, u32[]{:S(2)}, u32[]{:S(2)}) async-start(bf16[32,2,2048]{2,0,1:T(8,128)(2,1)} %bitcast.202), calls=%async_computation.1 | async-start | bytes 524288 | tf_op jit(solution)/shard_map/all_to_all | solution.py:219
  34.5 12.3 %copy-start.53 = (bf16[128,2048]{1,0:T(8,128)(2,1)S(1)}, bf16[128,2048]{1,0:T(8,128)(2,1)}, u32[]{:S(2)}) copy-start(bf16[128,2048]{1,0:T(8,128)(2,1)} %param.15) | copy-start | bytes 1572868
  34.5 12.6 %copy-start.54 = (bf16[128,2048]{1,0:T(8,128)(2,1)S(1)}, bf16[128,2048]{1,0:T(8,128)(2,1)}, u32[]{:S(2)}) copy-start(bf16[128,2048]{1,0:T(8,128)(2,1)} %param.19) | copy-start | bytes 1572868
  34.5 231.3 %all-to-all-start.2 = ((bf16[64,64,2048]{2,1,0:T(8,128)(2,1)}), bf16[64,64,2048]{2,1,0:T(8,128)(2,1)}, u32[]{:S(2)}, u32[]{:S(2)}) async-start(bf16[64,64,2048]{2,1,0:T(8,128)(2,1)} %stack.11), calls=%async_computation.2 | async-start | bytes 33554432 | tf_op jit(solution)/shard_map/all_to_all | solution.py:223
  51.3 223.9 %copy-start.15 = (bf16[128,2048]{0,1:T(8,128)(2,1)}, bf16[128,2048]{0,1:T(8,128)(2,1)S(1)}, u32[]{:S(2)}) copy-start(bf16[128,2048]{0,1:T(8,128)(2,1)S(1)} %copy.304) | copy-start | bytes 1572868
  305.4 55.0 %all-to-all-start.3 = ((bf16[64,2,6144]{2,1,0:T(2,128)(2,1)}), bf16[64,2,6144]{2,1,0:T(2,128)(2,1)S(1)}, u32[]{:S(2)}, u32[]{:S(2)}) async-start(bf16[64,2,6144]{2,1,0:T(2,128)(2,1)} %reshape.357), calls=%async_computation.3 | async-start | bytes 3145728 | tf_op jit(solution)/shard_map/all_to_all | solution.py:41
  632.4 7.4 copy-start.4
  632.4 7.4 copy-start.32
  632.4 7.4 copy-start.33
  650.8 36.5 %all-to-all-start.4 = ((f32[2,64,4096]{2,0,1:T(2,128)}), f32[2,64,4096]{2,0,1:T(2,128)S(1)}, u32[]{:S(2)}, u32[]{:S(2)}) async-start(f32[2,64,4096]{2,0,1:T(2,128)} %copy.351), calls=%async_computation.4 | async-start | bytes 4194304 | tf_op jit(solution)/shard_map/all_to_all | solution.py:263
  657.5 27.6 %collective-permute-start.3 = (bf16[127,2048]{1,0:T(8,128)(2,1)S(1)}, bf16[127,2048]{1,0:T(8,128)(2,1)S(1)}, u32[]{:S(2)}, u32[]{:S(2)}) collective-permute-start(bf16[127,2048]{1,0:T(8,128)(2,1)S(1)} %slice.29), channel_id=1, source_target_pairs={{0,2},{2,4},{4,6},{6,8},{8,10},{10,12},{12,14},{14,16},{16,18},{18... | collective-permute-start | bytes 1560584 | tf_op jit(solution)/shard_map/ppermute | solution.py:15
  697.7 56.2 %collective-permute-start = (bf16[127,2048]{0,1:T(8,128)(2,1)S(1)}, bf16[127,2048]{0,1:T(8,128)(2,1)}, u32[]{:S(2)}, u32[]{:S(2)}) collective-permute-start(bf16[127,2048]{0,1:T(8,128)(2,1)S(1)} %bitcast.276), channel_id=1, source_target_pairs={{2,0},{4,2},{6,4},{8,6},{10,8},{12,10},{14,12},{16,14},{18,16},{20... | collective-permute-start | bytes 1560584 | tf_op jit(solution)/shard_map/ppermute | solution.py:15
  718.8 23.3 %copy-start.51 = (bf16[128,2048]{0,1:T(8,128)(2,1)S(1)}, bf16[128,2048]{0,1:T(8,128)(2,1)}, u32[]{:S(2)}) copy-start(bf16[128,2048]{0,1:T(8,128)(2,1)} %get-tuple-element.71) | copy-start | bytes 1572868
  722.6 20.4 %copy-start.34 = (f32[1,128,64,32]{1,3,2,0:T(8,128)S(1)}, f32[1,128,64,32]{1,3,2,0:T(8,128)}, u32[]{:S(2)}) copy-start(f32[1,128,64,32]{1,3,2,0:T(8,128)} %get-tuple-element.64) | copy-start | bytes 3145732
  723.8 22.3 %all-to-all-start.7 = ((bf16[64,2,2048]{2,1,0:T(2,128)(2,1)}), bf16[64,2,2048]{2,1,0:T(2,128)(2,1)S(1)}, u32[]{:S(2)}, u32[]{:S(2)}) async-start(bf16[64,2,2048]{2,1,0:T(2,128)(2,1)} %reshape.359), calls=%async_computation.7 | async-start | bytes 1048576 | tf_op jit(solution)/shard_map/all_to_all | solution.py:62
  735.0 5.1 collective-permute-start.2
  759.1 19.9 %copy-start.52 = (bf16[1,134,2048]{2,1,0:T(8,128)(2,1)S(1)}, bf16[1,134,2048]{2,1,0:T(8,128)(2,1)}, u32[]{:S(2)}) copy-start(bf16[1,134,2048]{2,1,0:T(8,128)(2,1)} %maximum_bitcast_fusion.4) | copy-start | bytes 1646596
  776.6 14.7 %collective-permute-start.1 = (bf16[6,2048]{1,0:T(8,128)(2,1)S(1)}, bf16[6,2048]{1,0:T(8,128)(2,1)S(1)}, u32[]{:S(2)}, u32[]{:S(2)}) collective-permute-start(bf16[6,2048]{1,0:T(8,128)(2,1)S(1)} %bitcast.298), channel_id=1, source_target_pairs={{2,0},{4,2},{6,4},{8,6},{10,8},{12,10},{14,12},{16,14},{18,16},{20... | collective-permute-start | bytes 73736 | tf_op jit(solution)/shard_map/ppermute | solution.py:15
  783.0 16.5 %all-to-all-start.5 = ((bf16[64,1,224]{2,1,0:T(2,128)(2,1)}), bf16[64,1,224]{2,1,0:T(2,128)(2,1)S(1)}, u32[]{:S(2)}, u32[]{:S(2)}) async-start(bf16[64,1,224]{2,1,0:T(2,128)(2,1)} %all_to_all.64), calls=%async_computation.5 | async-start | bytes 131072 | tf_op jit(solution)/shard_map/all_to_all | solution.py:62
  791.4 13.4 %copy-start.55 = (bf16[7,2048]{1,0:T(8,128)(2,1)S(1)}, bf16[7,2048]{1,0:T(8,128)(2,1)}, u32[]{:S(2)}) copy-start(bf16[7,2048]{1,0:T(8,128)(2,1)} %param.20) | copy-start | bytes 86020
  791.4 13.4 %copy-start.56 = (pred[8,17]{0,1:T(8,128)(4,1)S(1)}, pred[8,17]{0,1:T(8,128)(4,1)}, u32[]{:S(2)}) copy-start(pred[8,17]{0,1:T(8,128)(4,1)} %constant.132) | copy-start | bytes 412
  800.3 12.8 %all-to-all-start.6 = ((bf16[64,1,224]{2,1,0:T(2,128)(2,1)}), bf16[64,1,224]{2,1,0:T(2,128)(2,1)S(1)}, u32[]{:S(2)}, u32[]{:S(2)}) async-start(bf16[64,1,224]{2,1,0:T(2,128)(2,1)} %broadcast_in_dim.26), calls=%async_computation.6 | async-start | bytes 131072 | tf_op jit(solution)/shard_map/all_to_all | solution.py:26
  813.1 16.8 %all-to-all-start.8 = ((bf16[64,2,2048]{2,1,0:T(2,128)(2,1)}), bf16[64,2,2048]{2,1,0:T(2,128)(2,1)S(1)}, u32[]{:S(2)}, u32[]{:S(2)}) async-start(bf16[64,2,2048]{2,1,0:T(2,128)(2,1)} %reshape.361), calls=%async_computation.8 | async-start | bytes 1048576 | tf_op jit(solution)/shard_map/all_to_all | solution.py:26
  (45 other events, 120.0 us)
